TPU v7x, 128 devices: a whole 4x4x4 slice. The times are simulated.
128 devices in a mesh: req: 16 (over y, x), exp: 8 (over z, core).
Axes of the slice: x: 4, y: 4, z: 4, core: 2. Of those that a mesh axis runs over, the one named last changes fastest.
Arguments:
- attention_out: bfloat16 [2048, 4096], P('req'), may hold values from -6 to 6
- residual: bfloat16 [2048, 4096], P('req', 'exp'), may hold values from -6 to 6
- w_out: bfloat16 [4096, 4096], P('req', 'exp'), may hold values from -0.09375 to 0.09375
- router_w: float32 [4096, 8], P('exp'), may hold values from -0.09375 to 0.09375
- norm_gain: float32 [4096], P('exp'), may hold values from 0.5 to 1.5
- page_pool: bfloat16 [4096, 8, 2048], P('req', None, 'exp'), may hold values from -6 to 6
- page_table: int32 [2048, 2], P('req'), may hold values from 0 to 255, as said below
- cache_len: int32 [2048], P('req'), may hold values from 1 to 16
- came_from: int32 [2048], replicated, may hold values from 0 to 2047, as said below
- routes: int32 [2048, 2], P('req'), may hold values from 0 to 7, all different within a row; in each aligned block of 128 rows (0 to 127, 128 to 255, ...) at most 64 rows name the same one
- w_gate: bfloat16 [16, 4096, 7168], P('req', None, 'exp'), as said below
- w_up: bfloat16 [16, 4096, 7168], P('req', None, 'exp'), as said below
- w_down: bfloat16 [16, 7168, 4096], P('req', 'exp'), as said below
Outputs:
- mixed: float32 [2048, 4096], P('req', 'exp')
- new_pages: bfloat16 [2048, 2, 8, 2048], P('req', None, None, 'exp')
Inputs may be any that keep to these rules, and one draw needn't show every extreme that they name: page_table's entries for the requests of one req group are distinct. came_from is a permutation; from each req group 4 rows go to each of the other 15 groups, each group receives 4 rows from each of them, and all other rows keep their place. `routes`: within the rows of one req group every expert is named by at most 64 rows, and some expert by exactly 64 rows in some group. `w_gate`: slices e and e + 8 along the first dimension are equal. `w_up`: slices e and e + 8 along the first dimension are equal. `w_down`: slices e and e + 8 along the first dimension are equal.
All inputs are finite; a program needn't handle non-finite values.
Results may differ from a plain program's by a relative error of at most 0.0055.
Values may be sent and summed in bfloat16 or wider, within the bound.
A program may use at most 128 MiB of HBM per device.

v0:
```python
import jax
import jax.numpy as jnp
from jax import lax
from jax.sharding import PartitionSpec as P

D = 4096
CAP = 32
MIG_PAIR = 4
EPSILON = 1e-05


def pick_rows(source, row_index, live_slot):
    taken_rows = jnp.take(source, row_index, axis=0)
    return jnp.where(live_slot[:, None], taken_rows, jnp.zeros((), source.dtype))


def body(
    attention_out,
    residual,
    w_out,
    router_w,
    norm_gain,
    page_pool,
    page_table,
    cache_len,
    came_from,
    routes,
    w_gate,
    w_up,
    w_down,
):
    groups = lax.axis_size("req")
    own_group = lax.axis_index("req")
    row_req = attention_out.shape[0]
    rows_all = came_from.shape[0]
    pages_req = page_table.shape[1]
    page_len = page_pool.shape[1]
    kv_slice = page_pool.shape[2]
    experts = groups // 2
    targets = jnp.arange(groups, dtype=jnp.int32)
    local_ids = jnp.arange(row_req, dtype=jnp.int32)
    dest_of = (
        jnp.zeros((rows_all,), jnp.int32).at[came_from].set(jnp.arange(rows_all, dtype=jnp.int32))
    )
    dest_group = dest_of // row_req
    dest_hot = (
        (dest_group[:, None] == targets[None, :]).astype(jnp.int32).reshape(groups, row_req, groups)
    )
    pair_rank = jnp.sum((jnp.cumsum(dest_hot, axis=1) - dest_hot) * dest_hot, axis=2).reshape(
        rows_all
    )
    own_dest = lax.dynamic_slice_in_dim(dest_group, own_group * row_req, row_req)
    own_rank = lax.dynamic_slice_in_dim(pair_rank, own_group * row_req, row_req)
    chosen_send = (
        (own_dest[None, None, :] == targets[:, None, None])
        & (own_rank[None, None, :] == jnp.arange(MIG_PAIR, dtype=jnp.int32)[None, :, None])
        & (targets[:, None, None] != own_group)
    )
    send_index = jnp.sum(jnp.where(chosen_send, local_ids[None, None, :], 0), axis=2).reshape(-1)
    send_live = jnp.any(chosen_send, axis=2).reshape(-1)
    moved_attn, moved_resid = (
        lax.all_to_all(
            pick_rows(attention_out, send_index, send_live),
            "req",
            split_axis=0,
            concat_axis=0,
            tiled=True,
        ),
        lax.all_to_all(
            pick_rows(residual, send_index, send_live),
            "req",
            split_axis=0,
            concat_axis=0,
            tiled=True,
        ),
    )
    new_source = lax.dynamic_slice_in_dim(came_from, own_group * row_req, row_req)
    source_group = new_source // row_req
    stays_home = source_group == own_group
    arrival = jnp.where(
        stays_home,
        new_source - own_group * row_req,
        row_req + source_group * MIG_PAIR + jnp.take(pair_rank, new_source),
    )
    attn_new = jnp.take(jnp.concatenate([attention_out, moved_attn], axis=0), arrival, axis=0)
    resid_new = jnp.take(jnp.concatenate([residual, moved_resid], axis=0), arrival, axis=0)
    projected = jnp.dot(
        attn_new,
        lax.all_gather(w_out, "req", axis=0, tiled=True),
        preferred_element_type=jnp.float32,
    )
    hidden = resid_new.astype(jnp.float32) + projected
    squares = jnp.sum(hidden * hidden, axis=1)
    scaled = hidden * norm_gain[None, :]
    raw_logits = jnp.dot(scaled, router_w, precision=lax.Precision.HIGHEST)
    row_stats = lax.psum(jnp.concatenate([squares[:, None], raw_logits], axis=1), "exp")
    total_sq = row_stats[:, 0]
    inverse = lax.rsqrt(total_sq / D + EPSILON)
    normed = scaled * inverse[:, None]
    logits = row_stats[:, 1:] * inverse[:, None]
    normed_rows = normed.astype(jnp.bfloat16)
    expert_ids = jnp.arange(experts, dtype=jnp.int32)
    chosen = jnp.sum(
        jnp.where(routes[:, :, None] == expert_ids[None, None, :], logits[:, None, :], 0.0), axis=2
    )
    gate_first = jax.nn.sigmoid(chosen[:, 0] - chosen[:, 1])
    gate_second = jax.nn.sigmoid(chosen[:, 1] - chosen[:, 0])
    flat_routes = routes.reshape(-1)
    expert_hot = (flat_routes[:, None] == expert_ids[None, :]).astype(jnp.int32)
    expert_rank = jnp.sum((jnp.cumsum(expert_hot, axis=0) - expert_hot) * expert_hot, axis=1)
    target_dev = flat_routes + experts * (expert_rank % 2)
    slot_index = expert_rank // 2
    assign_ids = jnp.arange(flat_routes.shape[0], dtype=jnp.int32)
    chosen_slot = (target_dev[None, None, :] == targets[:, None, None]) & (
        slot_index[None, None, :] == jnp.arange(CAP, dtype=jnp.int32)[None, :, None]
    )
    slot_source = jnp.sum(
        jnp.where(chosen_slot, assign_ids[None, None, :] // 2, 0), axis=2
    ).reshape(-1)
    slot_live = jnp.any(chosen_slot, axis=2).reshape(-1)
    outgoing = pick_rows(normed_rows, slot_source, slot_live)
    arrived = lax.all_to_all(outgoing, "req", split_axis=0, concat_axis=0, tiled=True)
    rows_full = lax.all_gather(arrived, "exp", axis=1, tiled=True)
    gate_h = jnp.dot(rows_full, w_gate[0], preferred_element_type=jnp.float32)
    up_h = jnp.dot(rows_full, w_up[0], preferred_element_type=jnp.float32)
    active = (jax.nn.silu(gate_h) * up_h).astype(jnp.bfloat16)
    partial_value = lax.optimization_barrier(
        jnp.dot(active, w_down[0], preferred_element_type=jnp.float32).astype(jnp.bfloat16)
    )
    partial_value, page_pool = lax.optimization_barrier((partial_value, page_pool))
    summed_value = lax.psum_scatter(partial_value, "exp", scatter_dimension=1, tiled=True)
    page_rows = jnp.take(page_pool, page_table.reshape(-1), axis=0).reshape(
        row_req, pages_req, page_len, kv_slice
    )
    position = (
        jnp.arange(pages_req, dtype=jnp.int32)[:, None] * page_len
        + jnp.arange(page_len, dtype=jnp.int32)[None, :]
    )
    kept_mask = position[None, :, :] < cache_len[:, None, None]
    page_rows = jnp.where(kept_mask[..., None], page_rows, jnp.zeros((), page_rows.dtype)).reshape(
        row_req, -1
    )
    moved_pages = lax.all_to_all(
        pick_rows(page_rows, send_index, send_live), "req", split_axis=0, concat_axis=0, tiled=True
    )
    new_pages = jnp.take(
        jnp.concatenate([page_rows, moved_pages], axis=0), arrival, axis=0
    ).reshape(row_req, pages_req, page_len, kv_slice)
    lookup = target_dev * CAP + slot_index
    returned = lax.all_to_all(summed_value, "req", split_axis=0, concat_axis=0, tiled=True)
    taken_rows = jnp.take(returned, lookup, axis=0).reshape(row_req, 2, -1).astype(jnp.float32)
    expert_part = gate_first[:, None] * taken_rows[:, 0] + gate_second[:, None] * taken_rows[:, 1]
    mixed = hidden + expert_part
    return (mixed, new_pages)


def solution(mesh):
    in_specs = (
        P("req", None),
        P("req", "exp"),
        P("req", "exp"),
        P("exp", None),
        P("exp"),
        P("req", None, "exp"),
        P("req", None),
        P("req"),
        P(),
        P("req", None),
        P("req", None, "exp"),
        P("req", None, "exp"),
        P("req", "exp", None),
    )
    out_specs = (P("req", "exp"), P("req", None, None, "exp"))
    return jax.shard_map(body, mesh=mesh, in_specs=in_specs, out_specs=out_specs, check_vma=False)
```

profile of v0, /device:TPU:0, one launch (start us, length us, event | category | flops | bytes accessed | tf_op | source)
XLA Modules:
  0.0 224.9 jit_solution(11997066119131765174)
XLA Ops:
  7.2 0.7 all-gather.3.cloned.1.call-update
  7.9 0.7 compare_select_fusion.1
  8.6 8.0 %scatter_custom_fusion = s32[2048]{0:T(1024)S(1)} fusion(s32[2048]{0:T(1024)S(1)} %compare_select_fusion.1, s32[2048]{0:T(1024)S(1)} %iota.72, s32[]{:T(128)} %constant.182.clone.1), kind=kCustom, calls=%fused_computation.93 | custom fusion | bytes 8196 | tf_op jit(solution)/shard_map/scatter | solution.py:43
  16.8 2.8 %select_reduce_fusion = s32[16,128]{0,1:T(8,128)S(1)} fusion(s32[16,128]{0,1:T(8,128)S(1)} %copy.115), kind=kOutput, calls=%fused_computation.27 | output fusion | flops 4388864 | bytes 16384 | tf_op jit(solution)/shard_map/jit(cumsum)/reduce_window_sum | solution.py:49
  19.9 0.2 select_reduce_fusion.1
  20.2 0.2 fusion.30
  20.6 1.6 gather_fusion.1
  22.4 0.8 select_select_fusion.4
  23.1 7.1 %all-to-all-start = ((bf16[16,4,512]{2,1,0:T(4,128)(2,1)}), bf16[16,4,512]{2,1,0:T(4,128)(2,1)S(1)}, u32[]{:S(2)}, u32[]{:S(2)}) async-start(bf16[16,4,512]{2,1,0:T(4,128)(2,1)} %select_select_fusion.4), calls=%async_computation | async-start | bytes 131072 | tf_op jit(solution)/shard_map/all_to_all | solution.py:69
  30.4 0.8 copy.122
  31.4 0.1 reshape.526
  31.6 0.9 gather_fusion.6
  32.4 0.1 select_select_fusion.2
  32.6 1.0 all_to_all.38
  33.6 0.8 compare_select_fusion.15
  34.3 1.1 gather_fusion
  35.5 0.6 reduce-window.6
  36.1 0.2 slice_reduce_fusion
  36.5 0.4 fusion.19
  36.9 0.8 compare_and_fusion.5
  37.7 0.3 all-to-all-done
  38.0 7.0 %all-to-all-start.1 = ((bf16[16,4,4096]{2,1,0:T(4,128)(2,1)}), bf16[16,4,4096]{2,1,0:T(4,128)(2,1)S(1)}, u32[]{:S(2)}, u32[]{:S(2)}) async-start(bf16[16,4,4096]{2,1,0:T(4,128)(2,1)} %all_to_all.38), calls=%async_computation.1 | async-start | bytes 1048576 | tf_op jit(solution)/shard_map/all_to_all | solution.py:62
  45.1 0.4 and_reduce_fusion
  45.5 0.8 gather_fusion.2
  46.3 16.4 %all-to-all-done.1 = bf16[16,4,4096]{2,1,0:T(4,128)(2,1)S(1)} async-done(((bf16[16,4,4096]{2,1,0:T(4,128)(2,1)}), bf16[16,4,4096]{2,1,0:T(4,128)(2,1)S(1)}, u32[]{:S(2)}, u32[]{:S(2)}) %all-to-all-start.1) | async-done | bytes 524320 | tf_op jit(solution)/shard_map/all_to_all | solution.py:62
  62.9 1.4 pad_maximum_fusion
  64.2 2.2 gather_fusion.7
  66.4 3.4 %all-gather.3.cloned.1.call-done = bf16[4096,512]{1,0:T(8,128)(2,1)} async-done(((bf16[256,512]{1,0:T(8,128)(2,1)}), bf16[4096,512]{1,0:T(8,128)(2,1)}) %all-gather.3.cloned.1.call-update) | async-done | bytes 4194320 | tf_op jit(solution)/shard_map/all_gather | solution.py:89
  69.8 3.4 %multiply_reduce_fusion = (f32[128]{0:T(128)S(1)}, f32[128,512]{1,0:T(8,128)S(1)}) fusion(bf16[4096,512]{1,0:T(8,128)(2,1)} %all-gather.3.cloned.1.call-done, bf16[128,4096]{1,0:T(8,128)(2,1)} %gather_fusion.7, pred[128]{0:T(512)(128)(4,1)S(1)} %get-tuple-element.8, bf16[128,512]{1,0:T(8,128)(2,1)S(1)} %gather_fusion.2), kind=kOutput, calls=%fused_computation.48 | convolution fusion | flops 537722752 | bytes 5636736 | tf_op jit(solution)/shard_map/dot_general | solution.py:87
  73.2 0.3 fusion.27
  73.5 15.1 %psum.7 = f32[128,9]{0,1:T(8,128)S(1)} all-reduce(f32[128,9]{0,1:T(8,128)S(1)} %pad_maximum_fusion.3), channel_id=1, replica_groups=mesh['req'=16,'exp'=8] {'exp'}, use_global_device_ids=true, to_apply=%region_6.9 | all-reduce | flops 1152 | bytes 9216 | tf_op jit(solution)/shard_map/psum | solution.py:96
  88.7 2.0 gather_fusion.3
  90.7 0.2 select_select_fusion.3
  90.9 15.3 %all_to_all.54 = bf16[16,32,512]{2,1,0:T(8,128)(2,1)} all-to-all(bf16[16,32,512]{2,1,0:T(8,128)(2,1)S(1)} %select_select_fusion.3), channel_id=1, replica_groups=mesh['req'=16,'exp'=8] {'req'}, dimensions={0} | all-to-all | bytes 1048576 | tf_op jit(solution)/shard_map/all_to_all | solution.py:122
  106.2 0.2 reduce-scatter.2.cloned.1.call-start
  106.4 28.4 %all-gather.5.cloned.1.call-done = bf16[512,4096]{1,0:T(8,128)(2,1)} async-done(((bf16[512,512]{1,0:T(8,128)(2,1)}), bf16[512,4096]{1,0:T(8,128)(2,1)}) %all-gather.5.cloned.1.call-update) | async-done | bytes 4194320 | tf_op jit(solution)/shard_map/all_gather | solution.py:123
  134.9 9.8 %fusion.4 = f32[512,896]{1,0:T(8,128)S(1)} fusion(bf16[512,4096]{1,0:T(8,128)(2,1)} %all-gather.5.cloned.1.call-done, bf16[1,4096,896]{2,1,0:T(8,128)(2,1)} %param.27), kind=kOutput, calls=%fused_computation.15 | convolution fusion | flops 3758096384 | bytes 13369344 | tf_op jit(solution)/shard_map/dot_general | solution.py:124
  144.7 16.2 %fusion.6 = bf16[512,4096]{1,0:T(8,128)(2,1)} fusion(bf16[1,896,4096]{2,1,0:T(8,128)(2,1)} %param.29, f32[512,896]{1,0:T(8,128)S(1)} %fusion.4, bf16[512,4096]{1,0:T(8,128)(2,1)} %all-gather.5.cloned.1.call-done, bf16[1,4096,896]{2,1,0:T(8,128)(2,1)} %param.28), kind=kOutput, calls=%fused_computation.17 | convolution fusion | flops 7521042432 | bytes 24903680 | tf_op jit(solution)/shard_map/dot_general | solution.py:128
  161.1 0.1 reduce_sum.63
  161.2 0.4 copy-done.7
  161.7 0.1 reshape.530
  161.9 0.2 broadcast_compare_fusion
  162.1 0.4 broadcast_in_dim.231
  162.6 1.1 copy.132
  163.7 0.1 copy.130
  163.8 0.4 broadcast_in_dim.233
  164.3 1.1 copy.133
  165.6 0.8 gather_fusion.5
  166.3 0.5 gather.47
  166.9 1.4 select_select_fusion
  168.3 0.9 gather_fusion.8
  169.2 0.1 select_select_fusion.1
  169.3 1.0 all_to_all.46
  170.3 6.8 %all-to-all-start.4 = ((bf16[16,4,4096]{2,1,0:T(4,128)(2,1)}), bf16[16,4,4096]{2,1,0:T(4,128)(2,1)S(1)}, u32[]{:S(2)}, u32[]{:S(2)}) async-start(bf16[16,4,4096]{2,1,0:T(4,128)(2,1)} %all_to_all.46), calls=%async_computation.5 | async-start | bytes 1048576 | tf_op jit(solution)/shard_map/all_to_all | solution.py:143
  177.2 11.9 %all-to-all-done.4 = bf16[16,4,4096]{2,1,0:T(4,128)(2,1)S(1)} async-done(((bf16[16,4,4096]{2,1,0:T(4,128)(2,1)}), bf16[16,4,4096]{2,1,0:T(4,128)(2,1)S(1)}, u32[]{:S(2)}, u32[]{:S(2)}) %all-to-all-start.4) | async-done | bytes 524320 | tf_op jit(solution)/shard_map/all_to_all | solution.py:143
  189.2 1.4 pad_maximum_fusion.1
  190.6 2.2 gather_fusion.9
  192.8 6.6 %reduce-scatter.2.cloned.1.call-done = bf16[512,512]{1,0:T(8,128)(2,1)} async-done(((bf16[512,4096]{1,0:T(8,128)(2,1)}), bf16[512,512]{1,0:T(8,128)(2,1)}) %reduce-scatter.2.cloned.1.call-update) | async-done | bytes 524304 | tf_op jit(solution)/shard_map/reduce_scatter | solution.py:131
  199.3 6.7 %all-to-all-start.3 = ((bf16[16,32,512]{2,1,0:T(8,128)(2,1)}), bf16[16,32,512]{2,1,0:T(8,128)(2,1)S(1)}, u32[]{:S(2)}, u32[]{:S(2)}) async-start(bf16[16,32,512]{2,1,0:T(8,128)(2,1)} %bitcast.81), calls=%async_computation.4 | async-start | bytes 1048576 | tf_op jit(solution)/shard_map/all_to_all | solution.py:150
  206.0 1.4 broadcast_select_fusion
  207.4 1.2 copy.134
  208.6 7.5 %all-to-all-done.3 = bf16[16,32,512]{2,1,0:T(8,128)(2,1)S(1)} async-done(((bf16[16,32,512]{2,1,0:T(8,128)(2,1)}), bf16[16,32,512]{2,1,0:T(8,128)(2,1)S(1)}, u32[]{:S(2)}, u32[]{:S(2)}) %all-to-all-start.3) | async-done | bytes 524320 | tf_op jit(solution)/shard_map/all_to_all | solution.py:150
  216.1 1.2 gather_fusion.4
  217.5 0.8 fusion.24
  (81 shorter events, 2.6 us)
Async XLA Ops:
  7.2 158.4 %copy-start = (bf16[256,8,256]{2,1,0:T(8,128)(2,1)S(1)}, bf16[256,8,256]{2,1,0:T(8,128)(2,1)}, u32[]{:S(2)}) copy-start(bf16[256,8,256]{2,1,0:T(8,128)(2,1)} %param.22) | copy-start | bytes 3145732
  7.2 24.4 %copy-start.2 = (bf16[128,4096]{1,0:T(8,128)(2,1)S(1)}, bf16[128,4096]{1,0:T(8,128)(2,1)}, u32[]{:S(2)}) copy-start(bf16[128,4096]{1,0:T(8,128)(2,1)} %param.17) | copy-start | bytes 3145732
  7.2 62.6 %all-gather.3.cloned.1.call-start = ((), (), s32[]{:S(2)}) async-start(), calls=%async_computation.6 | async-start | bytes 4456448 | tf_op jit(solution)/shard_map/all_gather | solution.py:89
  23.1 14.9 %all-to-all-start = ((bf16[16,4,512]{2,1,0:T(4,128)(2,1)}), bf16[16,4,512]{2,1,0:T(4,128)(2,1)S(1)}, u32[]{:S(2)}, u32[]{:S(2)}) async-start(bf16[16,4,512]{2,1,0:T(4,128)(2,1)} %select_select_fusion.4), calls=%async_computation | async-start | bytes 131072 | tf_op jit(solution)/shard_map/all_to_all | solution.py:69
  31.5 13.9 %copy-start.3 = (bf16[128,512]{1,0:T(8,128)(2,1)S(1)}, bf16[128,512]{1,0:T(8,128)(2,1)}, u32[]{:S(2)}) copy-start(bf16[128,512]{1,0:T(8,128)(2,1)} %param.18) | copy-start | bytes 393220
  38.0 24.7 %all-to-all-start.1 = ((bf16[16,4,4096]{2,1,0:T(4,128)(2,1)}), bf16[16,4,4096]{2,1,0:T(4,128)(2,1)S(1)}, u32[]{:S(2)}, u32[]{:S(2)}) async-start(bf16[16,4,4096]{2,1,0:T(4,128)(2,1)} %all_to_all.38), calls=%async_computation.1 | async-start | bytes 1048576 | tf_op jit(solution)/shard_map/all_to_all | solution.py:62
  45.0 89.9 %all-gather.5.cloned.1.call-start = ((), (), s32[]{:S(2)}) async-start(), calls=%async_computation.7 | async-start | bytes 4718592 | tf_op jit(solution)/shard_map/all_gather | solution.py:123
  66.4 6.8 %copy-start.4 = (f32[512,8]{0,1:T(8,128)S(1)}, f32[512,8]{0,1:T(8,128)}, u32[]{:S(2)}) copy-start(f32[512,8]{0,1:T(8,128)} %param.20) | copy-start | bytes 49156
  66.4 6.8 %copy-start.6 = (f32[512]{0:T(512)S(1)}, f32[512]{0:T(512)}, u32[]{:S(2)}) copy-start(f32[512]{0:T(512)} %param.21) | copy-start | bytes 6148
  106.2 93.1 %reduce-scatter.2.cloned.1.call-start = ((), (), s32[]{:S(2)}) async-start(), calls=%async_computation.8 | async-start | bytes 4718592 | tf_op jit(solution)/shard_map/reduce_scatter | solution.py:131
  160.9 0.7 copy-start.7
  160.9 1.0 copy-start.8
  160.9 4.6 %copy-start.5 = (s32[128,2]{0,1:T(2,128)S(1)}, s32[128,2]{0,1:T(2,128)}, u32[]{:S(2)}) copy-start(s32[128,2]{0,1:T(2,128)} %param.26) | copy-start | bytes 3076
  168.3 20.8 %copy-start.1 = (bf16[128,4096]{1,0:T(8,128)(2,1)}, bf16[128,4096]{1,0:T(8,128)(2,1)S(1)}, u32[]{:S(2)}) copy-start(bf16[128,4096]{1,0:T(8,128)(2,1)S(1)} %select_select_fusion) | copy-start | bytes 3145732
  170.3 18.8 %all-to-all-start.4 = ((bf16[16,4,4096]{2,1,0:T(4,128)(2,1)}), bf16[16,4,4096]{2,1,0:T(4,128)(2,1)S(1)}, u32[]{:S(2)}, u32[]{:S(2)}) async-start(bf16[16,4,4096]{2,1,0:T(4,128)(2,1)} %all_to_all.46), calls=%async_computation.5 | async-start | bytes 1048576 | tf_op jit(solution)/shard_map/all_to_all | solution.py:143
  199.3 16.8 %all-to-all-start.3 = ((bf16[16,32,512]{2,1,0:T(8,128)(2,1)}), bf16[16,32,512]{2,1,0:T(8,128)(2,1)S(1)}, u32[]{:S(2)}, u32[]{:S(2)}) async-start(bf16[16,32,512]{2,1,0:T(8,128)(2,1)} %bitcast.81), calls=%async_computation.4 | async-start | bytes 1048576 | tf_op jit(solution)/shard_map/all_to_all | solution.py:150
Sparse Core Ops, SparseCore 0:
  10.2 59.6 all-gather.2
  106.3 28.4 all-gather.4
  161.1 38.2 reduce-scatter.1
where the time goes:
time: 226 us; the launch traced here: 225 us
  waiting for transfers between devices  75.2 us (33%)
  local copies, waits for them, and re-layouts  32.2 us (14%)
  blocking collectives  30.4 us (13%)
  matrix products  29.7 us (13%)
  starting transfers between devices  27.9 us (12%)
  other arithmetic  15.3 us (7%)
  between operations  14.3 us (6%)
    all_gather x1, waiting for transfers between devices, body(): rows_full = lax.all_gather(arrived, 'exp', axis=1, tiled=True)  28.4 us
    all_to_all x1, waiting for transfers between devices, body(): lax.all_to_all(pick_rows(attention_out, send_index, send_live), 'req', sp...  16.4 us
    dot_general x1, matrix products, body(): jnp.dot(active, w_down[0], preferred_element_type=jnp.float32)  16.2 us
    all_to_all x1, blocking collectives, body(): lax.all_to_all(outgoing, 'req', split_axis=0, concat_axis=0, tiled=True)  15.3 us
    psum x1, blocking collectives, body(): lax.psum(jnp.concatenate([squares[:, None], raw_logits], axis=1), 'exp')  15.1 us
    all_to_all x1, waiting for transfers between devices, body(): lax.all_to_all(pick_rows(page_rows, send_index, send_live), 'req', split_...  11.9 us
    dot_general x1, matrix products, body(): gate_h = jnp.dot(rows_full, w_gate[0], preferred_element_type=jnp.float32)  9.79 us
    scatter x1, local copies, waits for them, and re-layouts, body(): jnp.zeros((rows_all,), jnp.int32).at[came_from]  8.04 us
  transfers between devices with their start and end apart: 7, of which 7 were waited for; matrix products, arithmetic and copies ran while one was open for 18% of the time, Pallas kernels for 0%

commit v1 on v0

--- a/solution.py
+++ b/solution.py
@@ -120,7 +120,9 @@
     slot_live = jnp.any(chosen_slot, axis=2).reshape(-1)
     outgoing = pick_rows(normed_rows, slot_source, slot_live)
     arrived = lax.all_to_all(outgoing, "req", split_axis=0, concat_axis=0, tiled=True)
-    rows_full = lax.all_gather(arrived, "exp", axis=1, tiled=True)
+    rows_full = jnp.concatenate(
+        lax.all_to_all(jnp.stack([arrived] * lax.axis_size("exp")), "exp", 0, 0), axis=1
+    )
     gate_h = jnp.dot(rows_full, w_gate[0], preferred_element_type=jnp.float32)
     up_h = jnp.dot(rows_full, w_up[0], preferred_element_type=jnp.float32)
     active = (jax.nn.silu(gate_h) * up_h).astype(jnp.bfloat16)

time: 226 us -> 246 us (1.088)
  blocking collectives: 30.4 us -> 83.5 us
  waiting for transfers between devices: 75.2 us -> 44.9 us
  starting transfers between devices: 27.9 us -> 24.4 us
  local copies, waits for them, and re-layouts: 32.2 us -> 35.4 us
  matrix products: 29.7 us -> 27.2 us
    all_to_all x0 -> x1, blocking collectives: none -> 53.2 us  [body(): lax.all_to_all(jnp.stack([arrived] * lax.axis_size('exp')), 'exp', 0, 0)]
    all_gather x1 -> x0, waiting for transfers between devices: 28.4 us -> none  [body(): rows_full = lax.all_gather(arrived, 'exp', axis=1, tiled=True)]
    all_to_all x1, starting transfers between devices: 6.81 us -> 3.57 us  [body(): lax.all_to_all(pick_rows(page_rows, send_index, send_live), 'req', split_...]
    dot_general x1, matrix products: 9.79 us -> 7.2 us  [body(): gate_h = jnp.dot(rows_full, w_gate[0], preferred_element_type=jnp.float32)]
    unnamed x23 -> x27, local copies, waits for them, and re-layouts: 4.74 us -> 6.72 us
  transfers between devices with their start and end apart: 7 -> 6, of which waited for: 7 -> 6; matrix products, arithmetic and copies ran while one was open for 18% -> 17% of each run, Pallas kernels for 0% -> 0%
where the time goes in v1:
time: 246 us; the launch traced here: 245 us
  blocking collectives  83.5 us (34%)
  waiting for transfers between devices  44.9 us (18%)
  local copies, waits for them, and re-layouts  35.4 us (14%)
  matrix products  27.2 us (11%)
  starting transfers between devices  24.4 us (10%)
  other arithmetic  15.3 us (6%)
  between operations  14.6 us (6%)
    all_to_all x1, blocking collectives, body(): lax.all_to_all(jnp.stack([arrived] * lax.axis_size('exp')), 'exp', 0, 0)  53.2 us
    dot_general x1, matrix products, body(): jnp.dot(active, w_down[0], preferred_element_type=jnp.float32)  16.4 us
    all_to_all x1, waiting for transfers between devices, body(): lax.all_to_all(pick_rows(attention_out, send_index, send_live), 'req', sp...  15.7 us
    all_to_all x1, blocking collectives, body(): lax.all_to_all(outgoing, 'req', split_axis=0, concat_axis=0, tiled=True)  15.2 us
    psum x1, blocking collectives, body(): lax.psum(jnp.concatenate([squares[:, None], raw_logits], axis=1), 'exp')  15.1 us
    all_to_all x1, waiting for transfers between devices, body(): lax.all_to_all(pick_rows(page_rows, send_index, send_live), 'req', split_...  11.4 us
    scatter x1, local copies, waits for them, and re-layouts, body(): jnp.zeros((rows_all,), jnp.int32).at[came_from]  8.04 us
    all_to_all x1, waiting for transfers between devices, body(): lax.all_to_all(summed_value, 'req', split_axis=0, concat_axis=0, tiled=True)  7.51 us
  transfers between devices with their start and end apart: 6, of which 6 were waited for; matrix products, arithmetic and copies ran while one was open for 17% of the time, Pallas kernels for 0%

profile of v1, /device:TPU:0, one launch (start us, length us, event | category | flops | bytes accessed | tf_op | source)
XLA Modules:
  0.0 245.3 jit_solution(16116742093835065628)
XLA Ops:
  7.2 0.7 all-gather.2.cloned.1.call-update
  7.9 0.7 compare_select_fusion.1
  8.6 8.0 %scatter_custom_fusion = s32[2048]{0:T(1024)S(1)} fusion(s32[2048]{0:T(1024)S(1)} %compare_select_fusion.1, s32[2048]{0:T(1024)S(1)} %iota.72, s32[]{:T(128)} %constant.182.clone.1), kind=kCustom, calls=%fused_computation.94 | custom fusion | bytes 8196 | tf_op jit(solution)/shard_map/scatter | solution.py:43
  16.8 2.8 %select_reduce_fusion = s32[16,128]{0,1:T(8,128)S(1)} fusion(s32[16,128]{0,1:T(8,128)S(1)} %copy.119), kind=kOutput, calls=%fused_computation.27 | output fusion | flops 4388864 | bytes 16384 | tf_op jit(solution)/shard_map/jit(cumsum)/reduce_window_sum | solution.py:49
  19.9 0.2 select_reduce_fusion.1
  20.2 0.2 fusion.31
  20.6 1.6 gather_fusion.1
  22.4 0.8 select_select_fusion.4
  23.1 7.1 %all-to-all-start = ((bf16[16,4,512]{2,1,0:T(4,128)(2,1)}), bf16[16,4,512]{2,1,0:T(4,128)(2,1)S(1)}, u32[]{:S(2)}, u32[]{:S(2)}) async-start(bf16[16,4,512]{2,1,0:T(4,128)(2,1)} %select_select_fusion.4), calls=%async_computation | async-start | bytes 131072 | tf_op jit(solution)/shard_map/all_to_all | solution.py:69
  30.4 0.8 copy.126
  31.4 0.1 reshape.535
  31.6 0.9 gather_fusion.6
  32.4 0.1 select_select_fusion.2
  32.6 1.0 all_to_all.39
  33.6 0.8 compare_select_fusion.15
  34.3 1.1 gather_fusion
  35.5 0.6 reduce-window.6
  36.1 0.2 slice_reduce_fusion
  36.5 0.4 fusion.20
  36.9 0.8 compare_and_fusion.5
  37.7 0.3 all-to-all-done
  38.0 7.0 %all-to-all-start.1 = ((bf16[16,4,4096]{2,1,0:T(4,128)(2,1)}), bf16[16,4,4096]{2,1,0:T(4,128)(2,1)S(1)}, u32[]{:S(2)}, u32[]{:S(2)}) async-start(bf16[16,4,4096]{2,1,0:T(4,128)(2,1)} %all_to_all.39), calls=%async_computation.1 | async-start | bytes 1048576 | tf_op jit(solution)/shard_map/all_to_all | solution.py:62
  45.1 0.4 and_reduce_fusion
  45.5 1.5 gather_fusion.2
  47.0 15.7 %all-to-all-done.1 = bf16[16,4,4096]{2,1,0:T(4,128)(2,1)S(1)} async-done(((bf16[16,4,4096]{2,1,0:T(4,128)(2,1)}), bf16[16,4,4096]{2,1,0:T(4,128)(2,1)S(1)}, u32[]{:S(2)}, u32[]{:S(2)}) %all-to-all-start.1) | async-done | bytes 524320 | tf_op jit(solution)/shard_map/all_to_all | solution.py:62
  62.9 1.4 pad_maximum_fusion
  64.3 2.2 gather_fusion.7
  66.4 3.4 %all-gather.2.cloned.1.call-done = bf16[4096,512]{1,0:T(8,128)(2,1)} async-done(((bf16[256,512]{1,0:T(8,128)(2,1)}), bf16[4096,512]{1,0:T(8,128)(2,1)}) %all-gather.2.cloned.1.call-update) | async-done | bytes 4194320 | tf_op jit(solution)/shard_map/all_gather | solution.py:89
  69.8 3.4 %multiply_reduce_fusion = (f32[128]{0:T(128)S(1)}, f32[128,512]{1,0:T(8,128)S(1)}) fusion(bf16[4096,512]{1,0:T(8,128)(2,1)} %all-gather.2.cloned.1.call-done, bf16[128,4096]{1,0:T(8,128)(2,1)} %gather_fusion.7, pred[128]{0:T(512)(128)(4,1)S(1)} %get-tuple-element.8, bf16[128,512]{1,0:T(8,128)(2,1)S(1)} %copy-done.5), kind=kOutput, calls=%fused_computation.49 | convolution fusion | flops 537722752 | bytes 5636736 | tf_op jit(solution)/shard_map/dot_general | solution.py:87
  73.2 0.3 fusion.28
  73.5 15.1 %psum.7 = f32[128,9]{0,1:T(8,128)S(1)} all-reduce(f32[128,9]{0,1:T(8,128)S(1)} %pad_maximum_fusion.3), channel_id=1, replica_groups=mesh['req'=16,'exp'=8] {'exp'}, use_global_device_ids=true, to_apply=%region_6.9 | all-reduce | flops 1152 | bytes 9216 | tf_op jit(solution)/shard_map/psum | solution.py:96
  88.7 2.0 gather_fusion.3
  90.7 0.2 select_select_fusion.3
  90.9 15.2 %all_to_all.56 = bf16[16,32,512]{2,1,0:T(8,128)(2,1)S(1)} all-to-all(bf16[16,32,512]{2,1,0:T(8,128)(2,1)S(1)} %select_select_fusion.3), channel_id=1, replica_groups=mesh['req'=16,'exp'=8] {'req'}, dimensions={0} | all-to-all | bytes 1048576 | tf_op jit(solution)/shard_map/all_to_all | solution.py:122
  106.1 0.2 copy.132
  106.3 0.4 stack.5
  106.7 53.2 %all_to_all.57 = bf16[8,512,512]{1,2,0:T(8,128)(2,1)S(1)} all-to-all(bf16[8,512,512]{1,2,0:T(8,128)(2,1)S(1)} %stack.5), channel_id=1, replica_groups=mesh['req'=16,'exp'=8] {'exp'}, dimensions={0} | all-to-all | bytes 8388608 | tf_op jit(solution)/shard_map/all_to_all | solution.py:124
  159.9 2.0 copy-done.3
  161.8 7.2 %fusion.4 = f32[512,896]{1,0:T(8,128)S(1)} fusion(bf16[512,4096]{0,1:T(8,128)(2,1)S(1)} %bitcast.77, bf16[1,4096,896]{2,1,0:T(8,128)(2,1)} %param.27), kind=kOutput, calls=%fused_computation.15 | convolution fusion | flops 3758096384 | bytes 13369344 | tf_op jit(solution)/shard_map/dot_general | solution.py:126
  169.0 16.4 %fusion.6 = bf16[512,4096]{1,0:T(8,128)(2,1)} fusion(bf16[1,896,4096]{2,1,0:T(8,128)(2,1)} %param.29, f32[512,896]{1,0:T(8,128)S(1)} %fusion.4, bf16[512,4096]{0,1:T(8,128)(2,1)} %bitcast.78, bf16[1,4096,896]{2,1,0:T(8,128)(2,1)} %param.28), kind=kOutput, calls=%fused_computation.17 | convolution fusion | flops 7521042432 | bytes 24903680 | tf_op jit(solution)/shard_map/dot_general | solution.py:130
  185.8 0.4 copy-done.9
  186.5 0.2 broadcast_compare_fusion
  186.7 0.4 broadcast_in_dim.231
  187.1 1.1 copy.137
  188.2 0.1 copy.135
  188.4 0.4 broadcast_in_dim.233
  188.8 1.1 copy.138
  190.1 0.8 gather_fusion.5
  190.9 0.5 gather.47
  191.4 1.4 select_select_fusion
  192.8 0.9 gather_fusion.8
  193.7 0.1 select_select_fusion.1
  193.8 1.0 all_to_all.47
  194.9 3.6 %all-to-all-start.5 = ((bf16[16,4,4096]{2,1,0:T(4,128)(2,1)}), bf16[16,4,4096]{2,1,0:T(4,128)(2,1)S(1)}, u32[]{:S(2)}, u32[]{:S(2)}) async-start(bf16[16,4,4096]{2,1,0:T(4,128)(2,1)} %all_to_all.47), calls=%async_computation.6 | async-start | bytes 1048576 | tf_op jit(solution)/shard_map/all_to_all | solution.py:145
  198.5 11.4 %all-to-all-done.5 = bf16[16,4,4096]{2,1,0:T(4,128)(2,1)S(1)} async-done(((bf16[16,4,4096]{2,1,0:T(4,128)(2,1)}), bf16[16,4,4096]{2,1,0:T(4,128)(2,1)S(1)}, u32[]{:S(2)}, u32[]{:S(2)}) %all-to-all-start.5) | async-done | bytes 524320 | tf_op jit(solution)/shard_map/all_to_all | solution.py:145
  210.0 1.4 pad_maximum_fusion.1
  211.3 2.2 gather_fusion.9
  213.5 5.9 %reduce-scatter.2.cloned.1.call-done = bf16[512,512]{1,0:T(8,128)(2,1)} async-done(((bf16[512,4096]{1,0:T(8,128)(2,1)}), bf16[512,512]{1,0:T(8,128)(2,1)}) %reduce-scatter.2.cloned.1.call-update) | async-done | bytes 524304 | tf_op jit(solution)/shard_map/reduce_scatter | solution.py:133
  219.4 6.7 %all-to-all-start.4 = ((bf16[16,32,512]{2,1,0:T(8,128)(2,1)}), bf16[16,32,512]{2,1,0:T(8,128)(2,1)S(1)}, u32[]{:S(2)}, u32[]{:S(2)}) async-start(bf16[16,32,512]{2,1,0:T(8,128)(2,1)} %bitcast.86), calls=%async_computation.5 | async-start | bytes 1048576 | tf_op jit(solution)/shard_map/all_to_all | solution.py:152
  226.1 1.4 broadcast_select_fusion
  227.5 1.2 copy.139
  228.7 7.5 %all-to-all-done.4 = bf16[16,32,512]{2,1,0:T(8,128)(2,1)S(1)} async-done(((bf16[16,32,512]{2,1,0:T(8,128)(2,1)}), bf16[16,32,512]{2,1,0:T(8,128)(2,1)S(1)}, u32[]{:S(2)}, u32[]{:S(2)}) %all-to-all-start.4) | async-done | bytes 524320 | tf_op jit(solution)/shard_map/all_to_all | solution.py:152
  236.3 1.2 gather_fusion.4
  237.6 0.8 fusion.25
  (85 shorter events, 2.9 us)
Async XLA Ops:
  7.2 182.9 %copy-start = (bf16[256,8,256]{2,1,0:T(8,128)(2,1)S(1)}, bf16[256,8,256]{2,1,0:T(8,128)(2,1)}, u32[]{:S(2)}) copy-start(bf16[256,8,256]{2,1,0:T(8,128)(2,1)} %param.22) | copy-start | bytes 3145732
  7.2 24.4 %copy-start.2 = (bf16[128,4096]{1,0:T(8,128)(2,1)S(1)}, bf16[128,4096]{1,0:T(8,128)(2,1)}, u32[]{:S(2)}) copy-start(bf16[128,4096]{1,0:T(8,128)(2,1)} %param.17) | copy-start | bytes 3145732
  7.2 62.6 %all-gather.2.cloned.1.call-start = ((), (), s32[]{:S(2)}) async-start(), calls=%async_computation.7 | async-start | bytes 4456448 | tf_op jit(solution)/shard_map/all_gather | solution.py:89
  23.1 14.9 %all-to-all-start = ((bf16[16,4,512]{2,1,0:T(4,128)(2,1)}), bf16[16,4,512]{2,1,0:T(4,128)(2,1)S(1)}, u32[]{:S(2)}, u32[]{:S(2)}) async-start(bf16[16,4,512]{2,1,0:T(4,128)(2,1)} %select_select_fusion.4), calls=%async_computation | async-start | bytes 131072 | tf_op jit(solution)/shard_map/all_to_all | solution.py:69
  31.5 13.9 %copy-start.4 = (bf16[128,512]{1,0:T(8,128)(2,1)S(1)}, bf16[128,512]{1,0:T(8,128)(2,1)}, u32[]{:S(2)}) copy-start(bf16[128,512]{1,0:T(8,128)(2,1)} %param.18) | copy-start | bytes 393220
  38.0 24.7 %all-to-all-start.1 = ((bf16[16,4,4096]{2,1,0:T(4,128)(2,1)}), bf16[16,4,4096]{2,1,0:T(4,128)(2,1)S(1)}, u32[]{:S(2)}, u32[]{:S(2)}) async-start(bf16[16,4,4096]{2,1,0:T(4,128)(2,1)} %all_to_all.39), calls=%async_computation.1 | async-start | bytes 1048576 | tf_op jit(solution)/shard_map/all_to_all | solution.py:62
  45.0 174.4 %reduce-scatter.2.cloned.1.call-start = ((), (), s32[]{:S(2)}) async-start(), calls=%async_computation.8 | async-start | bytes 4718592 | tf_op jit(solution)/shard_map/reduce_scatter | solution.py:133
  64.2 5.6 %copy-start.5 = (bf16[128,512]{1,0:T(8,128)(2,1)S(1)}, bf16[128,512]{1,0:T(8,128)(2,1)}, u32[]{:S(2)}) copy-start(bf16[128,512]{1,0:T(8,128)(2,1)} %gather_fusion.2) | copy-start | bytes 393220
  66.4 6.8 %copy-start.6 = (f32[512,8]{0,1:T(8,128)S(1)}, f32[512,8]{0,1:T(8,128)}, u32[]{:S(2)}) copy-start(f32[512,8]{0,1:T(8,128)} %param.20) | copy-start | bytes 49156
  66.4 6.8 %copy-start.8 = (f32[512]{0:T(512)S(1)}, f32[512]{0:T(512)}, u32[]{:S(2)}) copy-start(f32[512]{0:T(512)} %param.21) | copy-start | bytes 6148
  159.9 2.0 copy-start.3
  185.4 0.7 copy-start.9
  185.4 1.0 copy-start.10
  185.4 4.6 %copy-start.7 = (s32[128,2]{0,1:T(2,128)S(1)}, s32[128,2]{0,1:T(2,128)}, u32[]{:S(2)}) copy-start(s32[128,2]{0,1:T(2,128)} %param.26) | copy-start | bytes 3076
  192.8 17.0 %copy-start.1 = (bf16[128,4096]{1,0:T(8,128)(2,1)}, bf16[128,4096]{1,0:T(8,128)(2,1)S(1)}, u32[]{:S(2)}) copy-start(bf16[128,4096]{1,0:T(8,128)(2,1)S(1)} %select_select_fusion) | copy-start | bytes 3145732
  194.9 15.0 %all-to-all-start.5 = ((bf16[16,4,4096]{2,1,0:T(4,128)(2,1)}), bf16[16,4,4096]{2,1,0:T(4,128)(2,1)S(1)}, u32[]{:S(2)}, u32[]{:S(2)}) async-start(bf16[16,4,4096]{2,1,0:T(4,128)(2,1)} %all_to_all.47), calls=%async_computation.6 | async-start | bytes 1048576 | tf_op jit(solution)/shard_map/all_to_all | solution.py:145
  219.4 16.8 %all-to-all-start.4 = ((bf16[16,32,512]{2,1,0:T(8,128)(2,1)}), bf16[16,32,512]{2,1,0:T(8,128)(2,1)S(1)}, u32[]{:S(2)}, u32[]{:S(2)}) async-start(bf16[16,32,512]{2,1,0:T(8,128)(2,1)} %bitcast.86), calls=%async_computation.5 | async-start | bytes 1048576 | tf_op jit(solution)/shard_map/all_to_all | solution.py:152
Sparse Core Ops, SparseCore 0:
  10.2 59.6 all-gather.1
  185.6 33.7 reduce-scatter.1
